TPU v7x, 32 devices: a whole 2x2x4 slice. The times are simulated.
32 devices in a mesh: col: 4 (over y, x), row: 8 (over z, core).
Axes of the slice: x: 2, y: 2, z: 4, core: 2. Of those that a mesh axis runs over, the one named last changes fastest.
Arguments:
- velocity: bfloat16 [4, 524288], P(None, ('col', 'row')), may hold values from -6 to 6
- pair_struct: int32 [4096], P(('col', 'row')), may hold values from 0 to 63
- pair_panel: int32 [4096], P(('col', 'row')), may hold values from 0 to 127
- pair_count: int32 [32], P(('col', 'row')), may hold values from 32 to 128, as said below
- mortar_coef: bfloat16 [4096, 128, 128], P(('col', 'row')), may hold values from -0.0625 to 0.0625
- bem_matrix: bfloat16 [32768, 32768], P('row', 'col'), may hold values from -0.03125 to 0.03125
- self_term: float32 [32768], P('row'), may hold values from 0.5 to 2
Outputs:
- pressure: bfloat16 [4, 32768], P(None, 'row')
- load: float32 [4, 524288], P(None, ('col', 'row'))
Inputs may be any that keep to these rules, and one draw needn't show every extreme that they name: pair_struct numbers a structural block within the slot's own device. `pair_count`: some device has all its slots live.
All inputs are finite; a program needn't handle non-finite values.
Results may differ from a plain program's by a relative error of at most 0.005.
Values may be sent and summed in bfloat16 or wider, within the bound.
No kernel may reach another device: no remote copies, remote signals or barrier semaphores. Data moves between devices by JAX's collectives and lax.ppermute only.
A program may use at most 128 MiB of HBM per device.

v0:
```python
import functools

import jax
import jax.numpy as jnp
from jax import lax
from jax.experimental import pallas as pl
from jax.experimental.pallas import tpu as pltpu
from jax.sharding import PartitionSpec as P


F32 = jnp.float32
BF16 = jnp.bfloat16
FORWARD_GROUP = 32
BACKWARD_GROUP = 64
HEAD_ROWS = 256
WINDOW_ROWS = 256
CHUNK_ROWS = 256
BODY_CHUNKS = 2
BUFFER_ROWS = 1536


def half_split(block, wide):
    src = lax.broadcasted_iota(jnp.int32, (wide, wide), 0)
    dst = lax.broadcasted_iota(jnp.int32, (wide, wide), 1)
    want = jnp.where(dst < block, 2 * dst, 2 * (dst - block) + 1)
    return jnp.where(src == want, 1.0, 0.0).astype(BF16)


def half_spread(block, part):
    src = lax.broadcasted_iota(jnp.int32, (block, 2 * block), 0)
    dst = lax.broadcasted_iota(jnp.int32, (block, 2 * block), 1)
    return jnp.where(dst == 2 * src + part, 1.0, 0.0).astype(BF16)


def unpack_parts(wide_rows, cases, block):
    nb = wide_rows.shape[0]
    both = jnp.concatenate([wide_rows, wide_rows], axis=1)
    flat = both.reshape(nb * 2 * cases, 2 * block).astype(BF16)
    out = jnp.dot(flat, half_split(block, 2 * block), preferred_element_type=F32)
    out = out.reshape(nb, 2 * cases, 2 * block)
    row = lax.broadcasted_iota(jnp.int32, (nb, 2 * cases, block), 1)
    return jnp.where(row < cases, out[:, :, :block], out[:, :, block:])


def forward_kernel(head_rows, count_ref, struct_hbm, panel_hbm, vel_hbm, coef_hbm, bem_hbm,
                   keep_ref, send_ref, head_ref, coef,
                   vel_ref, vel, acc, struct_ref, panel_ref,
                   sems, small_sems, head_sem):
    slots, block, _ = coef.shape
    cases = vel_ref.shape[0]
    nblk = vel.shape[0]
    chunks = slots // FORWARD_GROUP
    core = lax.rem(lax.axis_index("row"), 2)

    def fetch(i):
        part = pl.ds(i * FORWARD_GROUP, FORWARD_GROUP)
        return pltpu.make_async_copy(coef_hbm.at[part], coef.at[part], sems.at[i])

    small = [
        pltpu.make_async_copy(src, dst, small_sems.at[n])
        for n, (src, dst) in enumerate(
            [(vel_hbm, vel_ref), (struct_hbm, struct_ref), (panel_hbm, panel_ref)])
    ]
    head_copy = pltpu.make_async_copy(
        bem_hbm.at[pl.ds(0, head_rows)], head_ref.at[pl.ds(0, head_rows)], head_sem)
    for copy in small:
        copy.start()
    for i in range(chunks):
        fetch(i).start()
    head_copy.start()
    acc[...] = jnp.zeros_like(acc)
    wide = 2 * block
    small[0].wait()
    rows = jnp.stack(
        [vel_ref[:, b * wide:(b + 1) * wide].astype(F32) for b in range(nblk)], axis=0
    )
    vel[...] = unpack_parts(rows, cases, block)
    for copy in small[1:]:
        copy.wait()
    count = count_ref[0]
    zero = jnp.zeros((2 * cases, block), F32)

    def group(i, carry):
        fetch(i).wait()
        base = i * FORWARD_GROUP
        outs = []
        for j in range(0, FORWARD_GROUP, 2):
            qa, qb = base + j, base + j + 1
            va = jnp.where(qa < count, vel[struct_ref[qa]], 0.0)
            vb = jnp.where(qb < count, vel[struct_ref[qb]], 0.0)
            lhs = jnp.concatenate(
                [jnp.concatenate([va, zero], axis=1), jnp.concatenate([zero, vb], axis=1)], axis=0
            ).astype(BF16)
            rhs = jnp.concatenate([coef[qa], coef[qb]], axis=1)
            outs.append(lax.dot_general(lhs, rhs, (((1,), (1,)), ((), ())),
                                        preferred_element_type=F32))
        for j in range(0, FORWARD_GROUP, 2):
            out = outs[j // 2]
            acc[panel_ref[base + j]] += out[:2 * cases]
            acc[panel_ref[base + j + 1]] += out[2 * cases:]
        return carry

    lax.fori_loop(0, chunks, group, 0)
    cols, half = keep_ref.shape[0], keep_ref.shape[1]
    for k in range(cols):
        c = lax.axis_index("col") ^ k
        keep_ref[k] = acc[pl.ds((2 * c + core) * half, half)]
        send_ref[k] = acc[pl.ds((2 * c + 1 - core) * half, half)]
    head_copy.wait()


def fetch_kernel(start, count, after_ref, held_ref, bem_hbm, out_ref, sem):
    part = pl.ds(start, count)
    copy = pltpu.make_async_copy(bem_hbm.at[part], out_ref.at[part], sem)
    copy.start()
    copy.wait()


def fetch_rows(start, count, after, held, bem_matrix):
    hbm = pl.BlockSpec(memory_space=pl.ANY)
    vmem = pl.BlockSpec(memory_space=pltpu.VMEM)
    return pl.pallas_call(
        functools.partial(fetch_kernel, start, count),
        name="fetch_rows",
        out_shape=pltpu.VMEM(held.shape, BF16),
        in_specs=[hbm, vmem, hbm],
        out_specs=vmem,
        scratch_shapes=[pltpu.SemaphoreType.DMA],
        input_output_aliases={1: 0},
        compiler_params=pltpu.CompilerParams(vmem_limit_bytes=1 << 20),
        cost_estimate=pl.CostEstimate(
            flops=0, transcendentals=0, bytes_accessed=2 * count * held.shape[1]),
    )(after, held, in_hbm(bem_matrix))


def bem_kernel(ready, per, xa_ref, xb_ref, self_hbm, held_ref, bem_hbm, out_ref, tiles,
               xrow, self_ref, sems, self_sem):
    half, rows8, block = xa_ref.shape
    cases = rows8 // 2
    rows, width = bem_hbm.shape
    ring = sems.shape[0]
    chunk = tiles.shape[0] // ring
    chunks = rows // chunk
    tile = per * chunk
    row_id = lax.axis_index("row")
    core = lax.rem(row_id, 2)
    wide = 2 * block

    def fetch(i):
        slot = lax.rem(i, ring)
        to = pl.ds(pl.multiple_of(slot * chunk, chunk), chunk)
        return pltpu.make_async_copy(
            bem_hbm.at[pl.ds(pl.multiple_of(i * chunk, chunk), chunk)], tiles.at[to],
            sems.at[slot])

    self_copy = pltpu.make_async_copy(self_hbm, self_ref, self_sem)
    for i in range(ready, min(ready + 1, ring, chunks)):
        fetch(i).start()
    parts = jnp.concatenate([xa_ref[...], xb_ref[...]], axis=0).astype(F32)
    flat = parts.reshape(2 * half * rows8, block).astype(BF16)
    even = jnp.dot(flat, half_spread(block, 0), preferred_element_type=F32)
    odd = jnp.dot(flat, half_spread(block, 1), preferred_element_type=F32)
    line = lax.broadcasted_iota(jnp.int32, even.shape, 0)
    both = jnp.where(lax.rem(line, rows8) < cases, even, odd)
    both = both.reshape(2 * half, rows8, wide)
    for j in range(half):
        first = jnp.where(core == 0, both[j], both[half + j])
        second = jnp.where(core == 0, both[half + j], both[j])
        xrow[:, j * wide:(j + 1) * wide] = first.astype(BF16)
        xrow[:, (half + j) * wide:(half + j + 1) * wide] = second.astype(BF16)

    for i in range(ready + 1, min(ring, chunks)):
        fetch(i).start()
    self_copy.start()

    def step(i, carry):
        for n in range(per):
            @pl.when(i * per + n >= ready)
            def _(n=n):
                fetch(i * per + n).wait()

            @pl.when(jnp.logical_and(i >= 1, (i - 1) * per + n + ring < chunks))
            def _(n=n):
                fetch((i - 1) * per + n + ring).start()

        slot = lax.rem(i, ring // per)
        got = lax.dot_general(
            xrow[...], tiles[pl.ds(pl.multiple_of(slot * tile, tile), tile)],
            (((1,), (1,)), ((), ())), preferred_element_type=F32)
        out_ref[:, pl.ds(pl.multiple_of(i * tile, tile), tile)] = got[:cases] + got[cases:]
        return carry

    lax.fori_loop(0, chunks // per, step, 0)
    start = row_id * rows
    self_copy.wait()

    @pl.when(start // width == lax.axis_index("col"))
    def _():
        offset = pl.multiple_of(lax.rem(start, width), rows)
        own = xrow[:, pl.ds(offset, rows)].astype(F32)
        out_ref[...] += self_ref[...][None, :] * (own[:cases] + own[cases:])


def backward_kernel(ranks, struct_hbm, panel_hbm, count_ref, coef, *refs):
    pieces, scratch = refs[:ranks], refs[ranks:]
    out_ref, table, acc, struct_ref, panel_ref, sems = scratch
    small = [
        pltpu.make_async_copy(src, dst, sems.at[n])
        for n, (src, dst) in enumerate(
            [(struct_hbm, struct_ref), (panel_hbm, panel_ref)])
    ]
    for copy in small:
        copy.start()
    slots, block, _ = coef.shape
    nblk, rows8, _ = acc.shape
    cases = rows8 // 2
    wide = 2 * block
    me = lax.axis_index("row")
    per = pieces[0].shape[1] // wide
    for k in range(ranks):
        rows = jnp.stack(
            [pieces[k][:, b * wide:(b + 1) * wide].astype(F32) for b in range(per)], axis=0)
        table[pl.ds((me ^ k) * per, per)] = unpack_parts(rows, cases, block)
    acc[...] = jnp.zeros_like(acc)
    for copy in small:
        copy.wait()
    count = count_ref[0]

    def group(i, carry):
        base = i * BACKWARD_GROUP
        outs = []
        for j in range(0, BACKWARD_GROUP, 2):
            qa, qb = base + j, base + j + 1
            pa = jnp.where(qa < count, table[panel_ref[qa]], 0.0)
            pb = jnp.where(qb < count, table[panel_ref[qb]], 0.0)
            lhs = jnp.concatenate([pa, pb], axis=0).astype(BF16)
            rhs = jnp.concatenate([coef[qa], coef[qb]], axis=1)
            outs.append(jnp.dot(lhs, rhs, preferred_element_type=F32))
        for j in range(0, BACKWARD_GROUP, 2):
            out = outs[j // 2]
            acc[struct_ref[base + j]] += out[:rows8, :block]
            acc[struct_ref[base + j + 1]] += out[rows8:, block:]
        return carry

    lax.fori_loop(0, slots // BACKWARD_GROUP, group, 0)
    rest = acc[...].reshape(nblk * rows8, block)
    even = odd = None
    spread0, spread1 = half_spread(block, 0), half_spread(block, 1)
    for _ in range(3):
        piece = rest.astype(BF16)
        rest = rest - piece.astype(F32)
        e = jnp.dot(piece, spread0, preferred_element_type=F32)
        o = jnp.dot(piece, spread1, preferred_element_type=F32)
        even = e if even is None else even + e
        odd = o if odd is None else odd + o
    even = even.reshape(nblk, rows8, wide)
    odd = odd.reshape(nblk, rows8, wide)
    for b in range(nblk):
        out_ref[:, b * wide:(b + 1) * wide] = even[b, :cases] + odd[b, cases:]


def swap(value, axis, size, mask):
    return lax.ppermute(value, axis, [(i, i ^ mask) for i in range(size)])


def in_hbm(value):
    return pltpu.with_memory_space_constraint(value, pltpu.HBM)


def on_device(velocity, pair_struct, pair_panel, pair_count, mortar_coef, bem_matrix, self_term):
    cases = velocity.shape[0]
    slots, block, _ = mortar_coef.shape
    wide = 2 * block
    node_blocks = velocity.shape[1] // wide
    ncol, nrow = lax.axis_size("col"), lax.axis_size("row")
    rows, width = bem_matrix.shape
    panel_blocks = ncol * width // wide
    half = panel_blocks // (2 * ncol)
    rows8 = 2 * cases
    smem = pl.BlockSpec(memory_space=pltpu.SMEM)
    vmem = pl.BlockSpec(memory_space=pltpu.VMEM)
    hbm = pl.BlockSpec(memory_space=pl.ANY)

    head_rows = min(HEAD_ROWS, rows // 4)
    window_rows = min(WINDOW_ROWS, rows // 4)
    chunk_rows = min(CHUNK_ROWS, rows // 4)
    buffer_rows = min(BUFFER_ROWS, rows)
    keep, send, held, coef = pl.pallas_call(
        functools.partial(forward_kernel, head_rows),
        name="mortar_forward",
        out_shape=[
            jax.ShapeDtypeStruct((ncol, half, rows8, block), F32),
            jax.ShapeDtypeStruct((ncol, half, rows8, block), F32),
            pltpu.VMEM((buffer_rows, width), BF16),
            pltpu.VMEM(mortar_coef.shape, BF16),
        ],
        in_specs=[smem] + [hbm] * 5,
        out_specs=[vmem] * 4,
        scratch_shapes=[
            pltpu.VMEM(velocity.shape, BF16),
            pltpu.VMEM((node_blocks, rows8, block), F32),
            pltpu.VMEM((panel_blocks, rows8, block), F32),
            pltpu.SMEM(pair_struct.shape, jnp.int32),
            pltpu.SMEM(pair_panel.shape, jnp.int32),
            pltpu.SemaphoreType.DMA((slots // FORWARD_GROUP,)),
            pltpu.SemaphoreType.DMA((3,)),
            pltpu.SemaphoreType.DMA,
        ],
        compiler_params=pltpu.CompilerParams(vmem_limit_bytes=8 << 20),
    )(pair_count, *[in_hbm(a) for a in
                    (pair_struct, pair_panel, velocity, mortar_coef, bem_matrix)])

    chip = keep + swap(send, "row", nrow, 1)
    plane = chip[0]
    arrived = [swap(chip[k], "col", ncol, k) for k in range(1, ncol)]
    held = fetch_rows(head_rows, window_rows, chip, held, bem_matrix)
    for got in arrived:
        plane = plane + got
    sent = plane.astype(BF16)
    whole = plane
    arrived = [swap(sent, "row", nrow, 2 * k) for k in range(1, nrow // 2)]
    held = fetch_rows(head_rows + window_rows, window_rows, sent, held, bem_matrix)
    for got in arrived:
        whole = whole + got.astype(F32)
    xa = whole.astype(BF16)
    xb = swap(xa, "row", nrow, 1)

    partial_value, _ = pl.pallas_call(
        functools.partial(bem_kernel, (head_rows + 2 * window_rows) // chunk_rows, BODY_CHUNKS),
        name="bem_product",
        out_shape=[
            jax.ShapeDtypeStruct((cases, rows), F32),
            pltpu.VMEM((buffer_rows, width), BF16),
        ],
        in_specs=[vmem, vmem, hbm, vmem, hbm],
        out_specs=[vmem, vmem],
        scratch_shapes=[
            pltpu.VMEM((rows8, width), BF16),
            pltpu.VMEM((rows,), F32),
            pltpu.SemaphoreType.DMA((buffer_rows // chunk_rows,)),
            pltpu.SemaphoreType.DMA,
        ],
        input_output_aliases={3: 1},
        compiler_params=pltpu.CompilerParams(vmem_limit_bytes=8 << 20),
    )(xa, xb, in_hbm(self_term), held, in_hbm(bem_matrix))

    total = partial_value
    for got in [swap(partial_value, "col", ncol, k) for k in range(1, ncol)]:
        total = total + got
    pressure = total.astype(BF16)

    mine = [pressure] + [swap(pressure, "row", nrow, 2 * k) for k in range(1, nrow // 2)]
    pieces = []
    for got in mine:
        pieces.append(got)
        pieces.append(swap(got, "row", nrow, 1))

    load = pl.pallas_call(
        functools.partial(backward_kernel, nrow),
        name="mortar_backward",
        out_shape=jax.ShapeDtypeStruct((cases, node_blocks * wide), F32),
        in_specs=[hbm, hbm, smem, vmem] + [vmem] * nrow,
        out_specs=vmem,
        scratch_shapes=[
            pltpu.VMEM((panel_blocks, rows8, block), F32),
            pltpu.VMEM((node_blocks, rows8, block), F32),
            pltpu.SMEM(pair_struct.shape, jnp.int32),
            pltpu.SMEM(pair_panel.shape, jnp.int32),
            pltpu.SemaphoreType.DMA((2,)),
        ],
        compiler_params=pltpu.CompilerParams(vmem_limit_bytes=8 << 20),
    )(in_hbm(pair_struct), in_hbm(pair_panel), pair_count, coef, *pieces)
    return (pressure, load)


def solution(mesh):
    placed = (
        P(None, ("col", "row")),
        P(("col", "row")),
        P(("col", "row")),
        P(("col", "row")),
        P(("col", "row"), None, None),
        P("row", "col"),
        P("row"),
    )
    return jax.shard_map(
        on_device,
        mesh=mesh,
        in_specs=placed,
        out_specs=(P(None, "row"), P(None, ("col", "row"))),
        check_vma=False,
    )
```

profile of v0, /device:TPU:0, one launch (start us, length us, event | category | flops | bytes accessed | tf_op | source)
XLA Modules:
  0.0 66.0 jit_solution(8900506360824830061)
XLA Ops:
  1.3 3.6 %mortar_forward.1 = (f32[4,16,8,128]{3,2,1,0:T(8,128)S(1)}, f32[4,16,8,128]{3,2,1,0:T(8,128)S(1)}, bf16[1536,8192]{1,0:T(8,128)(2,1)S(1)}, bf16[128,128,128]{2,1,0:T(8,128)(2,1)S(1)}) custom-call(s32[1]{0:T(128)S(6)} %copy.15.count_ref, s32[128]{0:T(128)} %struct_hbm.3, s32[128]{0:T(128)} %panel_hbm.3, bf16[4,16384]{1,0:T(4,128)(2,1)} %vel_hbm.1, ...), custom_call_target="tpu_custom_call" | custom-call | tf_op jit(solution)/shard_map/mortar_forward/pallas_call | solution.py:288
  4.9 0.6 collective-permute-start
  5.4 1.2 %collective-permute-done = f32[4,16,8,128]{3,2,1,0:T(8,128)S(1)} collective-permute-done((f32[4,16,8,128]{3,2,1,0:T(8,128)S(1)}, f32[4,16,8,128]{3,2,1,0:T(8,128)S(1)}, u32[]{:S(2)}, u32[]{:S(2)}) %collective-permute-start) | collective-permute-done | bytes 262176 | tf_op jit(solution)/shard_map/ppermute | solution.py:263
  6.6 2.9 %collective-permute-start.1 = (f32[16,8,128]{2,1,0:T(8,128)S(1)}, f32[16,8,128]{2,1,0:T(8,128)S(1)}, u32[]{:S(2)}, u32[]{:S(2)}) collective-permute-start(f32[16,8,128]{2,1,0:T(8,128)S(1)} %get-tuple-element.14), channel_id=1, source_target_pairs={{0,8},{8,0},{16,24},{24,16},{1,9},{9,1},{17,25},{25,17},{2,10},{10... | collective-permute-start | bytes 196616 | tf_op jit(solution)/shard_map/ppermute | solution.py:263
  9.6 1.5 %collective-permute-start.3 = (f32[16,8,128]{2,1,0:T(8,128)S(1)}, f32[16,8,128]{2,1,0:T(8,128)S(1)}, u32[]{:S(2)}, u32[]{:S(2)}) collective-permute-start(f32[16,8,128]{2,1,0:T(8,128)S(1)} %get-tuple-element.15), channel_id=1, source_target_pairs={{0,24},{8,16},{16,8},{24,0},{1,25},{9,17},{17,9},{25,1},{2,26},{10... | collective-permute-start | bytes 196616 | tf_op jit(solution)/shard_map/ppermute | solution.py:263
  11.1 0.9 %collective-permute-done.1 = f32[16,8,128]{2,1,0:T(8,128)S(1)} collective-permute-done((f32[16,8,128]{2,1,0:T(8,128)S(1)}, f32[16,8,128]{2,1,0:T(8,128)S(1)}, u32[]{:S(2)}, u32[]{:S(2)}) %collective-permute-start.1) | collective-permute-done | bytes 65568 | tf_op jit(solution)/shard_map/ppermute | solution.py:263
  12.0 2.8 %collective-permute-done.3 = f32[16,8,128]{2,1,0:T(8,128)S(1)} collective-permute-done((f32[16,8,128]{2,1,0:T(8,128)S(1)}, f32[16,8,128]{2,1,0:T(8,128)S(1)}, u32[]{:S(2)}, u32[]{:S(2)}) %collective-permute-start.3) | collective-permute-done | bytes 65568 | tf_op jit(solution)/shard_map/ppermute | solution.py:263
  14.8 1.1 %collective-permute-done.2 = f32[16,8,128]{2,1,0:T(8,128)S(1)} collective-permute-done((f32[16,8,128]{2,1,0:T(8,128)S(1)}, f32[16,8,128]{2,1,0:T(8,128)S(1)}, u32[]{:S(2)}, u32[]{:S(2)}) %collective-permute-start.2) | collective-permute-done | bytes 65568 | tf_op jit(solution)/shard_map/ppermute | solution.py:263
  15.9 3.7 %collective-permute-start.6 = (bf16[16,8,128]{2,1,0:T(8,128)(2,1)S(1)}, bf16[16,8,128]{2,1,0:T(8,128)(2,1)S(1)}, u32[]{:S(2)}, u32[]{:S(2)}) collective-permute-start(bf16[16,8,128]{2,1,0:T(8,128)(2,1)S(1)} %get-tuple-element.12.after_ref), channel_id=1, source_target_pairs={{0,6},{1,7},{2,4},{3,5},{4,2},{5,3},{6,0},{7,1},{8,14},{9,15},{10,... | collective-permute-start | bytes 98312 | tf_op jit(solution)/shard_map/ppermute | solution.py:263
  19.6 0.8 %collective-permute-start.4 = (bf16[16,8,128]{2,1,0:T(8,128)(2,1)S(1)}, bf16[16,8,128]{2,1,0:T(8,128)(2,1)S(1)}, u32[]{:S(2)}, u32[]{:S(2)}) collective-permute-start(bf16[16,8,128]{2,1,0:T(8,128)(2,1)S(1)} %get-tuple-element.12.after_ref), channel_id=1, source_target_pairs={{0,2},{1,3},{2,0},{3,1},{4,6},{5,7},{6,4},{7,5},{8,10},{9,11},{10,... | collective-permute-start | bytes 98312 | tf_op jit(solution)/shard_map/ppermute | solution.py:263
  20.4 1.4 %collective-permute-done.6 = bf16[16,8,128]{2,1,0:T(8,128)(2,1)S(1)} collective-permute-done((bf16[16,8,128]{2,1,0:T(8,128)(2,1)S(1)}, bf16[16,8,128]{2,1,0:T(8,128)(2,1)S(1)}, u32[]{:S(2)}, u32[]{:S(2)}) %collective-permute-start.6) | collective-permute-done | bytes 32800 | tf_op jit(solution)/shard_map/ppermute | solution.py:263
  21.8 2.6 %collective-permute-done.5 = bf16[16,8,128]{2,1,0:T(8,128)(2,1)S(1)} collective-permute-done((bf16[16,8,128]{2,1,0:T(8,128)(2,1)S(1)}, bf16[16,8,128]{2,1,0:T(8,128)(2,1)S(1)}, u32[]{:S(2)}, u32[]{:S(2)}) %collective-permute-start.5) | collective-permute-done | bytes 32800 | tf_op jit(solution)/shard_map/ppermute | solution.py:263
  24.5 2.2 %fetch_rows.2.held_ref = bf16[1536,8192]{1,0:T(8,128)(2,1)S(1)} custom-call(f32[4,16,8,128]{3,2,1,0:T(8,128)S(1)} %add.30.after_ref, bf16[1536,8192]{1,0:T(8,128)(2,1)S(1)} %get-tuple-element.9.held_ref, bf16[4096,8192]{1,0:T(8,128)(2,1)} %bem_hbm.7), custom_call_target="tpu_custom_call", output_to_operand_aliasing={{}: (1, {})} | custom-call | bytes 4194304 | tf_op jit(solution)/shard_map/fetch_rows/pallas_call | solution.py:122
  26.7 2.2 %fetch_rows.3.held_ref = bf16[1536,8192]{1,0:T(8,128)(2,1)S(1)} custom-call(bf16[16,8,128]{2,1,0:T(8,128)(2,1)S(1)} %get-tuple-element.12.after_ref, bf16[1536,8192]{1,0:T(8,128)(2,1)S(1)} %fetch_rows.2.held_ref, bf16[4096,8192]{1,0:T(8,128)(2,1)} %bem_hbm.7), custom_call_target="tpu_custom_call", output_to_operand_aliasing={{}: (1, {})} | custom-call | bytes 4194304 | tf_op jit(solution)/shard_map/fetch_rows/pallas_call | solution.py:122
  28.9 19.2 %bem_product.1 = (f32[4,4096]{1,0:T(4,128)S(1)}, bf16[1536,8192]{1,0:T(8,128)(2,1)S(1)}) custom-call(bf16[16,8,128]{2,1,0:T(8,128)(2,1)S(1)} %add_convert_fusion.1.xa_ref, bf16[16,8,128]{2,1,0:T(8,128)(2,1)S(1)} %collective-permute-done.7.xb_ref, f32[4096]{0:T(1024)} %self_hbm.1, ...), custom_call_target="tpu_custom_call", output_to_operand_aliasing={{1}: (3, {})} | custom-call | tf_op jit(solution)/shard_map/bem_product/pallas_call | solution.py:328
  48.1 1.5 %collective-permute-start.10 = (f32[4,4096]{1,0:T(4,128)S(1)}, f32[4,4096]{1,0:T(4,128)S(1)}, u32[]{:S(2)}, u32[]{:S(2)}) collective-permute-start(f32[4,4096]{1,0:T(4,128)S(1)} %get-tuple-element.10), channel_id=1, source_target_pairs={{0,24},{8,16},{16,8},{24,0},{1,25},{9,17},{17,9},{25,1},{2,26},{10... | collective-permute-start | bytes 196616 | tf_op jit(solution)/shard_map/ppermute | solution.py:263
  49.6 1.2 %collective-permute-start.9 = (f32[4,4096]{1,0:T(4,128)S(1)}, f32[4,4096]{1,0:T(4,128)S(1)}, u32[]{:S(2)}, u32[]{:S(2)}) collective-permute-start(f32[4,4096]{1,0:T(4,128)S(1)} %get-tuple-element.10), channel_id=1, source_target_pairs={{0,16},{8,24},{16,0},{24,8},{1,17},{9,25},{17,1},{25,9},{2,18},{10... | collective-permute-start | bytes 196616 | tf_op jit(solution)/shard_map/ppermute | solution.py:263
  50.8 0.9 %collective-permute-start.8 = (f32[4,4096]{1,0:T(4,128)S(1)}, f32[4,4096]{1,0:T(4,128)S(1)}, u32[]{:S(2)}, u32[]{:S(2)}) collective-permute-start(f32[4,4096]{1,0:T(4,128)S(1)} %get-tuple-element.10), channel_id=1, source_target_pairs={{0,8},{8,0},{16,24},{24,16},{1,9},{9,1},{17,25},{25,17},{2,10},{10... | collective-permute-start | bytes 196616 | tf_op jit(solution)/shard_map/ppermute | solution.py:263
  51.7 2.0 %collective-permute-done.10 = f32[4,4096]{1,0:T(4,128)S(1)} collective-permute-done((f32[4,4096]{1,0:T(4,128)S(1)}, f32[4,4096]{1,0:T(4,128)S(1)}, u32[]{:S(2)}, u32[]{:S(2)}) %collective-permute-start.10) | collective-permute-done | bytes 65568 | tf_op jit(solution)/shard_map/ppermute | solution.py:263
  53.7 1.3 %collective-permute-done.9 = f32[4,4096]{1,0:T(4,128)S(1)} collective-permute-done((f32[4,4096]{1,0:T(4,128)S(1)}, f32[4,4096]{1,0:T(4,128)S(1)}, u32[]{:S(2)}, u32[]{:S(2)}) %collective-permute-start.9) | collective-permute-done | bytes 65568 | tf_op jit(solution)/shard_map/ppermute | solution.py:263
  55.2 1.5 %collective-permute-start.16 = (bf16[4,4096]{1,0:T(4,128)(2,1)S(1)}, bf16[4,4096]{1,0:T(4,128)(2,1)S(1)}, u32[]{:S(2)}, u32[]{:S(2)}) collective-permute-start(bf16[4,4096]{1,0:T(4,128)(2,1)S(1)} %add_convert_fusion.refs_0_), channel_id=1, source_target_pairs={{0,6},{1,7},{2,4},{3,5},{4,2},{5,3},{6,0},{7,1},{8,14},{9,15},{10,... | collective-permute-start | bytes 98312 | tf_op jit(solution)/shard_map/ppermute | solution.py:263
  56.7 0.6 collective-permute-start.14
  57.3 2.3 %collective-permute-start.12 = (bf16[4,4096]{1,0:T(4,128)(2,1)S(1)}, bf16[4,4096]{1,0:T(4,128)(2,1)S(1)}, u32[]{:S(2)}, u32[]{:S(2)}) collective-permute-start(bf16[4,4096]{1,0:T(4,128)(2,1)S(1)} %add_convert_fusion.refs_0_), channel_id=1, source_target_pairs={{0,2},{1,3},{2,0},{3,1},{4,6},{5,7},{6,4},{7,5},{8,10},{9,11},{10,... | collective-permute-start | bytes 98312 | tf_op jit(solution)/shard_map/ppermute | solution.py:263
  59.6 1.5 %collective-permute-done.16.refs_6_ = bf16[4,4096]{1,0:T(4,128)(2,1)S(1)} collective-permute-done((bf16[4,4096]{1,0:T(4,128)(2,1)S(1)}, bf16[4,4096]{1,0:T(4,128)(2,1)S(1)}, u32[]{:S(2)}, u32[]{:S(2)}) %collective-permute-start.16) | collective-permute-done | bytes 32800 | tf_op jit(solution)/shard_map/ppermute | solution.py:263
  61.2 0.3 collective-permute-done.14.refs_4_
  61.5 0.2 collective-permute-start.15
  61.7 0.2 collective-permute-done.12.refs_2_
  61.9 0.2 collective-permute-start.13
  62.0 0.3 collective-permute-done.17.refs_7_
  62.4 0.4 collective-permute-done.15.refs_5_
  62.7 0.4 collective-permute-done.13.refs_3_
  63.1 2.9 %mortar_backward.1 = f32[4,16384]{1,0:T(4,128)} custom-call(s32[128]{0:T(128)} %struct_hbm.3, s32[128]{0:T(128)} %panel_hbm.3, s32[1]{0:T(128)S(6)} %copy.15.count_ref, bf16[128,128,128]{2,1,0:T(8,128)(2,1)S(1)} %get-tuple-element.11.coef, bf16[4,4096]{1,0:T(4,128)(2,1)S(1)} %add_convert_fusion.refs_0_, bf16[4,4096]{1,0:T(4,128)(2,1)S(1)} %collective-permute-done.11.refs_1_, ...), custom_call_target="tpu_custom_call" | custom-call | tf_op jit(solution)/shard_map/mortar_backward/pallas_call | solution.py:358
  (16 shorter events, 0.4 us)
Async XLA Ops:
  4.9 1.7 %collective-permute-start = (f32[4,16,8,128]{3,2,1,0:T(8,128)S(1)}, f32[4,16,8,128]{3,2,1,0:T(8,128)S(1)}, u32[]{:S(2)}, u32[]{:S(2)}) collective-permute-start(f32[4,16,8,128]{3,2,1,0:T(8,128)S(1)} %get-tuple-element.8), channel_id=1, source_target_pairs={{0,1},{1,0},{2,3},{3,2},{4,5},{5,4},{6,7},{7,6},{8,9},{9,8},{10,11... | collective-permute-start | bytes 786440 | tf_op jit(solution)/shard_map/ppermute | solution.py:263
  6.6 5.3 %collective-permute-start.1 = (f32[16,8,128]{2,1,0:T(8,128)S(1)}, f32[16,8,128]{2,1,0:T(8,128)S(1)}, u32[]{:S(2)}, u32[]{:S(2)}) collective-permute-start(f32[16,8,128]{2,1,0:T(8,128)S(1)} %get-tuple-element.14), channel_id=1, source_target_pairs={{0,8},{8,0},{16,24},{24,16},{1,9},{9,1},{17,25},{25,17},{2,10},{10... | collective-permute-start | bytes 196616 | tf_op jit(solution)/shard_map/ppermute | solution.py:263
  9.6 5.2 %collective-permute-start.3 = (f32[16,8,128]{2,1,0:T(8,128)S(1)}, f32[16,8,128]{2,1,0:T(8,128)S(1)}, u32[]{:S(2)}, u32[]{:S(2)}) collective-permute-start(f32[16,8,128]{2,1,0:T(8,128)S(1)} %get-tuple-element.15), channel_id=1, source_target_pairs={{0,24},{8,16},{16,8},{24,0},{1,25},{9,17},{17,9},{25,1},{2,26},{10... | collective-permute-start | bytes 196616 | tf_op jit(solution)/shard_map/ppermute | solution.py:263
  11.1 4.8 %collective-permute-start.2 = (f32[16,8,128]{2,1,0:T(8,128)S(1)}, f32[16,8,128]{2,1,0:T(8,128)S(1)}, u32[]{:S(2)}, u32[]{:S(2)}) collective-permute-start(f32[16,8,128]{2,1,0:T(8,128)S(1)} %get-tuple-element.16), channel_id=1, source_target_pairs={{0,16},{8,24},{16,0},{24,8},{1,17},{9,25},{17,1},{25,9},{2,18},{10... | collective-permute-start | bytes 196616 | tf_op jit(solution)/shard_map/ppermute | solution.py:263
  15.9 5.9 %collective-permute-start.6 = (bf16[16,8,128]{2,1,0:T(8,128)(2,1)S(1)}, bf16[16,8,128]{2,1,0:T(8,128)(2,1)S(1)}, u32[]{:S(2)}, u32[]{:S(2)}) collective-permute-start(bf16[16,8,128]{2,1,0:T(8,128)(2,1)S(1)} %get-tuple-element.12.after_ref), channel_id=1, source_target_pairs={{0,6},{1,7},{2,4},{3,5},{4,2},{5,3},{6,0},{7,1},{8,14},{9,15},{10,... | collective-permute-start | bytes 98312 | tf_op jit(solution)/shard_map/ppermute | solution.py:263
  19.6 4.8 %collective-permute-start.5 = (bf16[16,8,128]{2,1,0:T(8,128)(2,1)S(1)}, bf16[16,8,128]{2,1,0:T(8,128)(2,1)S(1)}, u32[]{:S(2)}, u32[]{:S(2)}) collective-permute-start(bf16[16,8,128]{2,1,0:T(8,128)(2,1)S(1)} %get-tuple-element.12.after_ref), channel_id=1, source_target_pairs={{0,4},{1,5},{2,6},{3,7},{4,0},{5,1},{6,2},{7,3},{8,12},{9,13},{10,... | collective-permute-start | bytes 98312 | tf_op jit(solution)/shard_map/ppermute | solution.py:263
  19.6 4.8 %collective-permute-start.4 = (bf16[16,8,128]{2,1,0:T(8,128)(2,1)S(1)}, bf16[16,8,128]{2,1,0:T(8,128)(2,1)S(1)}, u32[]{:S(2)}, u32[]{:S(2)}) collective-permute-start(bf16[16,8,128]{2,1,0:T(8,128)(2,1)S(1)} %get-tuple-element.12.after_ref), channel_id=1, source_target_pairs={{0,2},{1,3},{2,0},{3,1},{4,6},{5,7},{6,4},{7,5},{8,10},{9,11},{10,... | collective-permute-start | bytes 98312 | tf_op jit(solution)/shard_map/ppermute | solution.py:263
  24.4 4.5 %collective-permute-start.7 = (bf16[16,8,128]{2,1,0:T(8,128)(2,1)S(1)}, bf16[16,8,128]{2,1,0:T(8,128)(2,1)S(1)}, u32[]{:S(2)}, u32[]{:S(2)}) collective-permute-start(bf16[16,8,128]{2,1,0:T(8,128)(2,1)S(1)} %add_convert_fusion.1.xa_ref), channel_id=1, source_target_pairs={{0,1},{1,0},{2,3},{3,2},{4,5},{5,4},{6,7},{7,6},{8,9},{9,8},{10,11... | collective-permute-start | bytes 98312 | tf_op jit(solution)/shard_map/ppermute | solution.py:263
  48.1 5.6 %collective-permute-start.10 = (f32[4,4096]{1,0:T(4,128)S(1)}, f32[4,4096]{1,0:T(4,128)S(1)}, u32[]{:S(2)}, u32[]{:S(2)}) collective-permute-start(f32[4,4096]{1,0:T(4,128)S(1)} %get-tuple-element.10), channel_id=1, source_target_pairs={{0,24},{8,16},{16,8},{24,0},{1,25},{9,17},{17,9},{25,1},{2,26},{10... | collective-permute-start | bytes 196616 | tf_op jit(solution)/shard_map/ppermute | solution.py:263
  49.6 5.4 %collective-permute-start.9 = (f32[4,4096]{1,0:T(4,128)S(1)}, f32[4,4096]{1,0:T(4,128)S(1)}, u32[]{:S(2)}, u32[]{:S(2)}) collective-permute-start(f32[4,4096]{1,0:T(4,128)S(1)} %get-tuple-element.10), channel_id=1, source_target_pairs={{0,16},{8,24},{16,0},{24,8},{1,17},{9,25},{17,1},{25,9},{2,18},{10... | collective-permute-start | bytes 196616 | tf_op jit(solution)/shard_map/ppermute | solution.py:263
  50.8 4.3 %collective-permute-start.8 = (f32[4,4096]{1,0:T(4,128)S(1)}, f32[4,4096]{1,0:T(4,128)S(1)}, u32[]{:S(2)}, u32[]{:S(2)}) collective-permute-start(f32[4,4096]{1,0:T(4,128)S(1)} %get-tuple-element.10), channel_id=1, source_target_pairs={{0,8},{8,0},{16,24},{24,16},{1,9},{9,1},{17,25},{25,17},{2,10},{10... | collective-permute-start | bytes 196616 | tf_op jit(solution)/shard_map/ppermute | solution.py:263
  55.1 10.9 %copy-start = (bf16[4,4096]{1,0:T(4,128)(2,1)}, bf16[4,4096]{1,0:T(4,128)(2,1)S(1)}, u32[]{:S(2)}) copy-start(bf16[4,4096]{1,0:T(4,128)(2,1)S(1)} %add_convert_fusion.refs_0_) | copy-start | bytes 98308
  55.2 6.0 %collective-permute-start.16 = (bf16[4,4096]{1,0:T(4,128)(2,1)S(1)}, bf16[4,4096]{1,0:T(4,128)(2,1)S(1)}, u32[]{:S(2)}, u32[]{:S(2)}) collective-permute-start(bf16[4,4096]{1,0:T(4,128)(2,1)S(1)} %add_convert_fusion.refs_0_), channel_id=1, source_target_pairs={{0,6},{1,7},{2,4},{3,5},{4,2},{5,3},{6,0},{7,1},{8,14},{9,15},{10,... | collective-permute-start | bytes 98312 | tf_op jit(solution)/shard_map/ppermute | solution.py:263
  56.7 4.8 %collective-permute-start.14 = (bf16[4,4096]{1,0:T(4,128)(2,1)S(1)}, bf16[4,4096]{1,0:T(4,128)(2,1)S(1)}, u32[]{:S(2)}, u32[]{:S(2)}) collective-permute-start(bf16[4,4096]{1,0:T(4,128)(2,1)S(1)} %add_convert_fusion.refs_0_), channel_id=1, source_target_pairs={{0,4},{1,5},{2,6},{3,7},{4,0},{5,1},{6,2},{7,3},{8,12},{9,13},{10,... | collective-permute-start | bytes 98312 | tf_op jit(solution)/shard_map/ppermute | solution.py:263
  57.3 4.5 %collective-permute-start.12 = (bf16[4,4096]{1,0:T(4,128)(2,1)S(1)}, bf16[4,4096]{1,0:T(4,128)(2,1)S(1)}, u32[]{:S(2)}, u32[]{:S(2)}) collective-permute-start(bf16[4,4096]{1,0:T(4,128)(2,1)S(1)} %add_convert_fusion.refs_0_), channel_id=1, source_target_pairs={{0,2},{1,3},{2,0},{3,1},{4,6},{5,7},{6,4},{7,5},{8,10},{9,11},{10,... | collective-permute-start | bytes 98312 | tf_op jit(solution)/shard_map/ppermute | solution.py:263
  59.6 2.4 %collective-permute-start.11 = (bf16[4,4096]{1,0:T(4,128)(2,1)S(1)}, bf16[4,4096]{1,0:T(4,128)(2,1)S(1)}, u32[]{:S(2)}, u32[]{:S(2)}) collective-permute-start(bf16[4,4096]{1,0:T(4,128)(2,1)S(1)} %add_convert_fusion.refs_0_), channel_id=1, source_target_pairs={{0,1},{1,0},{2,3},{3,2},{4,5},{5,4},{6,7},{7,6},{8,9},{9,8},{10,11... | collective-permute-start | bytes 98312 | tf_op jit(solution)/shard_map/ppermute | solution.py:263
  61.2 1.2 %collective-permute-start.17 = (bf16[4,4096]{1,0:T(4,128)(2,1)S(1)}, bf16[4,4096]{1,0:T(4,128)(2,1)S(1)}, u32[]{:S(2)}, u32[]{:S(2)}) collective-permute-start(bf16[4,4096]{1,0:T(4,128)(2,1)S(1)} %collective-permute-done.16.refs_6_), channel_id=1, source_target_pairs={{0,1},{1,0},{2,3},{3,2},{4,5},{5,4},{6,7},{7,6},{8,9},{9,8},{10,11... | collective-permute-start | bytes 98312 | tf_op jit(solution)/shard_map/ppermute | solution.py:263
  61.5 1.2 %collective-permute-start.15 = (bf16[4,4096]{1,0:T(4,128)(2,1)S(1)}, bf16[4,4096]{1,0:T(4,128)(2,1)S(1)}, u32[]{:S(2)}, u32[]{:S(2)}) collective-permute-start(bf16[4,4096]{1,0:T(4,128)(2,1)S(1)} %collective-permute-done.14.refs_4_), channel_id=1, source_target_pairs={{0,1},{1,0},{2,3},{3,2},{4,5},{5,4},{6,7},{7,6},{8,9},{9,8},{10,11... | collective-permute-start | bytes 98312 | tf_op jit(solution)/shard_map/ppermute | solution.py:263
  61.9 1.2 %collective-permute-start.13 = (bf16[4,4096]{1,0:T(4,128)(2,1)S(1)}, bf16[4,4096]{1,0:T(4,128)(2,1)S(1)}, u32[]{:S(2)}, u32[]{:S(2)}) collective-permute-start(bf16[4,4096]{1,0:T(4,128)(2,1)S(1)} %collective-permute-done.12.refs_2_), channel_id=1, source_target_pairs={{0,1},{1,0},{2,3},{3,2},{4,5},{5,4},{6,7},{7,6},{8,9},{9,8},{10,11... | collective-permute-start | bytes 98312 | tf_op jit(solution)/shard_map/ppermute | solution.py:263
where the time goes:
time: 66.2 us; the launch traced here: 66 us
  Pallas kernels  30.1 us (45%)
  starting transfers between devices  17.9 us (27%)
  waiting for transfers between devices  16.5 us (25%)
  between operations  1.37 us (2%)
    pallas_call x1, Pallas kernels, on_device(): pl.pallas_call(functools.partial(bem_kernel, (head_rows + 2 * window_rows...  19.2 us
    ppermute x18, starting transfers between devices, swap(): return lax.ppermute(value, axis, [(i, i ^ mask) for i in range(size)])  17.9 us
    ppermute x18, waiting for transfers between devices, swap(): return lax.ppermute(value, axis, [(i, i ^ mask) for i in range(size)])  16.5 us
    pallas_call x2, Pallas kernels, fetch_rows(): pl.pallas_call(functools.partial(fetch_kernel, start, count), name='fetch...  4.4 us
    pallas_call x1, Pallas kernels, on_device(): pl.pallas_call(functools.partial(forward_kernel, head_rows), name='mortar...  3.59 us
    pallas_call x1, Pallas kernels, on_device(): pl.pallas_call(functools.partial(backward_kernel, nrow), name='mortar_bac...  2.93 us
  transfers between devices with their start and end apart: 18, of which 15 were waited for; matrix products, arithmetic and copies ran while one was open for 0% of the time, Pallas kernels for 7%

commit v1 on v0

--- a/solution.py
+++ b/solution.py
@@ -11,11 +11,11 @@
 F32 = jnp.float32
 BF16 = jnp.bfloat16
 FORWARD_GROUP = 32
-BACKWARD_GROUP = 64
+BACKWARD_GROUP = 128
 HEAD_ROWS = 256
-WINDOW_ROWS = 256
-CHUNK_ROWS = 256
-BODY_CHUNKS = 2
+WINDOW_ROWS = 384
+CHUNK_ROWS = 128
+BODY_CHUNKS = 4
 BUFFER_ROWS = 1536
 
 
@@ -246,7 +246,7 @@
     rest = acc[...].reshape(nblk * rows8, block)
     even = odd = None
     spread0, spread1 = half_spread(block, 0), half_spread(block, 1)
-    for _ in range(3):
+    for _ in range(2):
         piece = rest.astype(BF16)
         rest = rest - piece.astype(F32)
         e = jnp.dot(piece, spread0, preferred_element_type=F32)

time: 66.2 us -> 66.6 us (level)
    pallas_call x2, Pallas kernels: 4.4 us -> 5.59 us  [fetch_rows(): pl.pallas_call(functools.partial(fetch_kernel, start, count), name='fetch...]
  transfers between devices with their start and end apart: 18 -> 18, of which waited for: 15 -> 15; matrix products, arithmetic and copies ran while one was open for 0% -> 0% of each run, Pallas kernels for 7% -> 8%
where the time goes in v1:
time: 66.6 us; the launch traced here: 66.4 us
  Pallas kernels  30.5 us (46%)
  starting transfers between devices  17.9 us (27%)
  waiting for transfers between devices  16.5 us (25%)
  between operations  1.37 us (2%)
    pallas_call x1, Pallas kernels, on_device(): pl.pallas_call(functools.partial(bem_kernel, (head_rows + 2 * window_rows...  18.7 us
    ppermute x18, starting transfers between devices, swap(): return lax.ppermute(value, axis, [(i, i ^ mask) for i in range(size)])  17.9 us
    ppermute x18, waiting for transfers between devices, swap(): return lax.ppermute(value, axis, [(i, i ^ mask) for i in range(size)])  16.5 us
    pallas_call x2, Pallas kernels, fetch_rows(): pl.pallas_call(functools.partial(fetch_kernel, start, count), name='fetch...  5.59 us
    pallas_call x1, Pallas kernels, on_device(): pl.pallas_call(functools.partial(forward_kernel, head_rows), name='mortar...  3.59 us
    pallas_call x1, Pallas kernels, on_device(): pl.pallas_call(functools.partial(backward_kernel, nrow), name='mortar_bac...  2.65 us
  transfers between devices with their start and end apart: 18, of which 15 were waited for; matrix products, arithmetic and copies ran while one was open for 0% of the time, Pallas kernels for 8%

profile of v1, /device:TPU:0, one launch (start us, length us, event | category | flops | bytes accessed | tf_op | source)
XLA Modules:
  0.0 66.4 jit_solution(919934325066758667)
XLA Ops:
  1.3 3.6 %mortar_forward.1 = (f32[4,16,8,128]{3,2,1,0:T(8,128)S(1)}, f32[4,16,8,128]{3,2,1,0:T(8,128)S(1)}, bf16[1536,8192]{1,0:T(8,128)(2,1)S(1)}, bf16[128,128,128]{2,1,0:T(8,128)(2,1)S(1)}) custom-call(s32[1]{0:T(128)S(6)} %copy.15.count_ref, s32[128]{0:T(128)} %struct_hbm.3, s32[128]{0:T(128)} %panel_hbm.3, bf16[4,16384]{1,0:T(4,128)(2,1)} %vel_hbm.1, ...), custom_call_target="tpu_custom_call" | custom-call | tf_op jit(solution)/shard_map/mortar_forward/pallas_call | solution.py:288
  4.9 0.6 collective-permute-start
  5.4 1.2 %collective-permute-done = f32[4,16,8,128]{3,2,1,0:T(8,128)S(1)} collective-permute-done((f32[4,16,8,128]{3,2,1,0:T(8,128)S(1)}, f32[4,16,8,128]{3,2,1,0:T(8,128)S(1)}, u32[]{:S(2)}, u32[]{:S(2)}) %collective-permute-start) | collective-permute-done | bytes 262176 | tf_op jit(solution)/shard_map/ppermute | solution.py:263
  6.6 2.9 %collective-permute-start.1 = (f32[16,8,128]{2,1,0:T(8,128)S(1)}, f32[16,8,128]{2,1,0:T(8,128)S(1)}, u32[]{:S(2)}, u32[]{:S(2)}) collective-permute-start(f32[16,8,128]{2,1,0:T(8,128)S(1)} %get-tuple-element.14), channel_id=1, source_target_pairs={{0,8},{8,0},{16,24},{24,16},{1,9},{9,1},{17,25},{25,17},{2,10},{10... | collective-permute-start | bytes 196616 | tf_op jit(solution)/shard_map/ppermute | solution.py:263
  9.6 1.5 %collective-permute-start.3 = (f32[16,8,128]{2,1,0:T(8,128)S(1)}, f32[16,8,128]{2,1,0:T(8,128)S(1)}, u32[]{:S(2)}, u32[]{:S(2)}) collective-permute-start(f32[16,8,128]{2,1,0:T(8,128)S(1)} %get-tuple-element.15), channel_id=1, source_target_pairs={{0,24},{8,16},{16,8},{24,0},{1,25},{9,17},{17,9},{25,1},{2,26},{10... | collective-permute-start | bytes 196616 | tf_op jit(solution)/shard_map/ppermute | solution.py:263
  11.1 0.9 %collective-permute-done.1 = f32[16,8,128]{2,1,0:T(8,128)S(1)} collective-permute-done((f32[16,8,128]{2,1,0:T(8,128)S(1)}, f32[16,8,128]{2,1,0:T(8,128)S(1)}, u32[]{:S(2)}, u32[]{:S(2)}) %collective-permute-start.1) | collective-permute-done | bytes 65568 | tf_op jit(solution)/shard_map/ppermute | solution.py:263
  12.0 2.8 %collective-permute-done.3 = f32[16,8,128]{2,1,0:T(8,128)S(1)} collective-permute-done((f32[16,8,128]{2,1,0:T(8,128)S(1)}, f32[16,8,128]{2,1,0:T(8,128)S(1)}, u32[]{:S(2)}, u32[]{:S(2)}) %collective-permute-start.3) | collective-permute-done | bytes 65568 | tf_op jit(solution)/shard_map/ppermute | solution.py:263
  14.8 1.1 %collective-permute-done.2 = f32[16,8,128]{2,1,0:T(8,128)S(1)} collective-permute-done((f32[16,8,128]{2,1,0:T(8,128)S(1)}, f32[16,8,128]{2,1,0:T(8,128)S(1)}, u32[]{:S(2)}, u32[]{:S(2)}) %collective-permute-start.2) | collective-permute-done | bytes 65568 | tf_op jit(solution)/shard_map/ppermute | solution.py:263
  15.9 3.7 %collective-permute-start.6 = (bf16[16,8,128]{2,1,0:T(8,128)(2,1)S(1)}, bf16[16,8,128]{2,1,0:T(8,128)(2,1)S(1)}, u32[]{:S(2)}, u32[]{:S(2)}) collective-permute-start(bf16[16,8,128]{2,1,0:T(8,128)(2,1)S(1)} %get-tuple-element.12.after_ref), channel_id=1, source_target_pairs={{0,6},{1,7},{2,4},{3,5},{4,2},{5,3},{6,0},{7,1},{8,14},{9,15},{10,... | collective-permute-start | bytes 98312 | tf_op jit(solution)/shard_map/ppermute | solution.py:263
  19.6 0.8 %collective-permute-start.4 = (bf16[16,8,128]{2,1,0:T(8,128)(2,1)S(1)}, bf16[16,8,128]{2,1,0:T(8,128)(2,1)S(1)}, u32[]{:S(2)}, u32[]{:S(2)}) collective-permute-start(bf16[16,8,128]{2,1,0:T(8,128)(2,1)S(1)} %get-tuple-element.12.after_ref), channel_id=1, source_target_pairs={{0,2},{1,3},{2,0},{3,1},{4,6},{5,7},{6,4},{7,5},{8,10},{9,11},{10,... | collective-permute-start | bytes 98312 | tf_op jit(solution)/shard_map/ppermute | solution.py:263
  20.4 1.4 %collective-permute-done.6 = bf16[16,8,128]{2,1,0:T(8,128)(2,1)S(1)} collective-permute-done((bf16[16,8,128]{2,1,0:T(8,128)(2,1)S(1)}, bf16[16,8,128]{2,1,0:T(8,128)(2,1)S(1)}, u32[]{:S(2)}, u32[]{:S(2)}) %collective-permute-start.6) | collective-permute-done | bytes 32800 | tf_op jit(solution)/shard_map/ppermute | solution.py:263
  21.8 2.6 %collective-permute-done.5 = bf16[16,8,128]{2,1,0:T(8,128)(2,1)S(1)} collective-permute-done((bf16[16,8,128]{2,1,0:T(8,128)(2,1)S(1)}, bf16[16,8,128]{2,1,0:T(8,128)(2,1)S(1)}, u32[]{:S(2)}, u32[]{:S(2)}) %collective-permute-start.5) | collective-permute-done | bytes 32800 | tf_op jit(solution)/shard_map/ppermute | solution.py:263
  24.5 2.8 %fetch_rows.2.held_ref = bf16[1536,8192]{1,0:T(8,128)(2,1)S(1)} custom-call(f32[4,16,8,128]{3,2,1,0:T(8,128)S(1)} %add.30.after_ref, bf16[1536,8192]{1,0:T(8,128)(2,1)S(1)} %get-tuple-element.9.held_ref, bf16[4096,8192]{1,0:T(8,128)(2,1)} %bem_hbm.7), custom_call_target="tpu_custom_call", output_to_operand_aliasing={{}: (1, {})} | custom-call | bytes 6291456 | tf_op jit(solution)/shard_map/fetch_rows/pallas_call | solution.py:122
  27.3 2.8 %fetch_rows.3.held_ref = bf16[1536,8192]{1,0:T(8,128)(2,1)S(1)} custom-call(bf16[16,8,128]{2,1,0:T(8,128)(2,1)S(1)} %get-tuple-element.12.after_ref, bf16[1536,8192]{1,0:T(8,128)(2,1)S(1)} %fetch_rows.2.held_ref, bf16[4096,8192]{1,0:T(8,128)(2,1)} %bem_hbm.7), custom_call_target="tpu_custom_call", output_to_operand_aliasing={{}: (1, {})} | custom-call | bytes 6291456 | tf_op jit(solution)/shard_map/fetch_rows/pallas_call | solution.py:122
  30.1 18.7 %bem_product.1 = (f32[4,4096]{1,0:T(4,128)S(1)}, bf16[1536,8192]{1,0:T(8,128)(2,1)S(1)}) custom-call(bf16[16,8,128]{2,1,0:T(8,128)(2,1)S(1)} %add_convert_fusion.1.xa_ref, bf16[16,8,128]{2,1,0:T(8,128)(2,1)S(1)} %collective-permute-done.7.xb_ref, f32[4096]{0:T(1024)} %self_hbm.1, ...), custom_call_target="tpu_custom_call", output_to_operand_aliasing={{1}: (3, {})} | custom-call | tf_op jit(solution)/shard_map/bem_product/pallas_call | solution.py:328
  48.8 1.5 %collective-permute-start.10 = (f32[4,4096]{1,0:T(4,128)S(1)}, f32[4,4096]{1,0:T(4,128)S(1)}, u32[]{:S(2)}, u32[]{:S(2)}) collective-permute-start(f32[4,4096]{1,0:T(4,128)S(1)} %get-tuple-element.10), channel_id=1, source_target_pairs={{0,24},{8,16},{16,8},{24,0},{1,25},{9,17},{17,9},{25,1},{2,26},{10... | collective-permute-start | bytes 196616 | tf_op jit(solution)/shard_map/ppermute | solution.py:263
  50.3 1.2 %collective-permute-start.9 = (f32[4,4096]{1,0:T(4,128)S(1)}, f32[4,4096]{1,0:T(4,128)S(1)}, u32[]{:S(2)}, u32[]{:S(2)}) collective-permute-start(f32[4,4096]{1,0:T(4,128)S(1)} %get-tuple-element.10), channel_id=1, source_target_pairs={{0,16},{8,24},{16,0},{24,8},{1,17},{9,25},{17,1},{25,9},{2,18},{10... | collective-permute-start | bytes 196616 | tf_op jit(solution)/shard_map/ppermute | solution.py:263
  51.5 0.9 %collective-permute-start.8 = (f32[4,4096]{1,0:T(4,128)S(1)}, f32[4,4096]{1,0:T(4,128)S(1)}, u32[]{:S(2)}, u32[]{:S(2)}) collective-permute-start(f32[4,4096]{1,0:T(4,128)S(1)} %get-tuple-element.10), channel_id=1, source_target_pairs={{0,8},{8,0},{16,24},{24,16},{1,9},{9,1},{17,25},{25,17},{2,10},{10... | collective-permute-start | bytes 196616 | tf_op jit(solution)/shard_map/ppermute | solution.py:263
  52.4 2.0 %collective-permute-done.10 = f32[4,4096]{1,0:T(4,128)S(1)} collective-permute-done((f32[4,4096]{1,0:T(4,128)S(1)}, f32[4,4096]{1,0:T(4,128)S(1)}, u32[]{:S(2)}, u32[]{:S(2)}) %collective-permute-start.10) | collective-permute-done | bytes 65568 | tf_op jit(solution)/shard_map/ppermute | solution.py:263
  54.4 1.3 %collective-permute-done.9 = f32[4,4096]{1,0:T(4,128)S(1)} collective-permute-done((f32[4,4096]{1,0:T(4,128)S(1)}, f32[4,4096]{1,0:T(4,128)S(1)}, u32[]{:S(2)}, u32[]{:S(2)}) %collective-permute-start.9) | collective-permute-done | bytes 65568 | tf_op jit(solution)/shard_map/ppermute | solution.py:263
  55.8 1.5 %collective-permute-start.16 = (bf16[4,4096]{1,0:T(4,128)(2,1)S(1)}, bf16[4,4096]{1,0:T(4,128)(2,1)S(1)}, u32[]{:S(2)}, u32[]{:S(2)}) collective-permute-start(bf16[4,4096]{1,0:T(4,128)(2,1)S(1)} %add_convert_fusion.refs_0_), channel_id=1, source_target_pairs={{0,6},{1,7},{2,4},{3,5},{4,2},{5,3},{6,0},{7,1},{8,14},{9,15},{10,... | collective-permute-start | bytes 98312 | tf_op jit(solution)/shard_map/ppermute | solution.py:263
  57.4 0.6 collective-permute-start.14
  58.0 2.3 %collective-permute-start.12 = (bf16[4,4096]{1,0:T(4,128)(2,1)S(1)}, bf16[4,4096]{1,0:T(4,128)(2,1)S(1)}, u32[]{:S(2)}, u32[]{:S(2)}) collective-permute-start(bf16[4,4096]{1,0:T(4,128)(2,1)S(1)} %add_convert_fusion.refs_0_), channel_id=1, source_target_pairs={{0,2},{1,3},{2,0},{3,1},{4,6},{5,7},{6,4},{7,5},{8,10},{9,11},{10,... | collective-permute-start | bytes 98312 | tf_op jit(solution)/shard_map/ppermute | solution.py:263
  60.3 1.5 %collective-permute-done.16.refs_6_ = bf16[4,4096]{1,0:T(4,128)(2,1)S(1)} collective-permute-done((bf16[4,4096]{1,0:T(4,128)(2,1)S(1)}, bf16[4,4096]{1,0:T(4,128)(2,1)S(1)}, u32[]{:S(2)}, u32[]{:S(2)}) %collective-permute-start.16) | collective-permute-done | bytes 32800 | tf_op jit(solution)/shard_map/ppermute | solution.py:263
  61.8 0.3 collective-permute-done.14.refs_4_
  62.2 0.2 collective-permute-start.15
  62.3 0.2 collective-permute-done.12.refs_2_
  62.5 0.2 collective-permute-start.13
  62.7 0.3 collective-permute-done.17.refs_7_
  63.0 0.4 collective-permute-done.15.refs_5_
  63.4 0.4 collective-permute-done.13.refs_3_
  63.7 2.7 %mortar_backward.1 = f32[4,16384]{1,0:T(4,128)} custom-call(s32[128]{0:T(128)} %struct_hbm.3, s32[128]{0:T(128)} %panel_hbm.3, s32[1]{0:T(128)S(6)} %copy.15.count_ref, bf16[128,128,128]{2,1,0:T(8,128)(2,1)S(1)} %get-tuple-element.11.coef, bf16[4,4096]{1,0:T(4,128)(2,1)S(1)} %add_convert_fusion.refs_0_, bf16[4,4096]{1,0:T(4,128)(2,1)S(1)} %collective-permute-done.11.refs_1_, ...), custom_call_target="tpu_custom_call" | custom-call | tf_op jit(solution)/shard_map/mortar_backward/pallas_call | solution.py:358
  (16 shorter events, 0.4 us)
Async XLA Ops:
  4.9 1.7 %collective-permute-start = (f32[4,16,8,128]{3,2,1,0:T(8,128)S(1)}, f32[4,16,8,128]{3,2,1,0:T(8,128)S(1)}, u32[]{:S(2)}, u32[]{:S(2)}) collective-permute-start(f32[4,16,8,128]{3,2,1,0:T(8,128)S(1)} %get-tuple-element.8), channel_id=1, source_target_pairs={{0,1},{1,0},{2,3},{3,2},{4,5},{5,4},{6,7},{7,6},{8,9},{9,8},{10,11... | collective-permute-start | bytes 786440 | tf_op jit(solution)/shard_map/ppermute | solution.py:263
  6.6 5.3 %collective-permute-start.1 = (f32[16,8,128]{2,1,0:T(8,128)S(1)}, f32[16,8,128]{2,1,0:T(8,128)S(1)}, u32[]{:S(2)}, u32[]{:S(2)}) collective-permute-start(f32[16,8,128]{2,1,0:T(8,128)S(1)} %get-tuple-element.14), channel_id=1, source_target_pairs={{0,8},{8,0},{16,24},{24,16},{1,9},{9,1},{17,25},{25,17},{2,10},{10... | collective-permute-start | bytes 196616 | tf_op jit(solution)/shard_map/ppermute | solution.py:263
  9.6 5.2 %collective-permute-start.3 = (f32[16,8,128]{2,1,0:T(8,128)S(1)}, f32[16,8,128]{2,1,0:T(8,128)S(1)}, u32[]{:S(2)}, u32[]{:S(2)}) collective-permute-start(f32[16,8,128]{2,1,0:T(8,128)S(1)} %get-tuple-element.15), channel_id=1, source_target_pairs={{0,24},{8,16},{16,8},{24,0},{1,25},{9,17},{17,9},{25,1},{2,26},{10... | collective-permute-start | bytes 196616 | tf_op jit(solution)/shard_map/ppermute | solution.py:263
  11.1 4.8 %collective-permute-start.2 = (f32[16,8,128]{2,1,0:T(8,128)S(1)}, f32[16,8,128]{2,1,0:T(8,128)S(1)}, u32[]{:S(2)}, u32[]{:S(2)}) collective-permute-start(f32[16,8,128]{2,1,0:T(8,128)S(1)} %get-tuple-element.16), channel_id=1, source_target_pairs={{0,16},{8,24},{16,0},{24,8},{1,17},{9,25},{17,1},{25,9},{2,18},{10... | collective-permute-start | bytes 196616 | tf_op jit(solution)/shard_map/ppermute | solution.py:263
  15.9 5.9 %collective-permute-start.6 = (bf16[16,8,128]{2,1,0:T(8,128)(2,1)S(1)}, bf16[16,8,128]{2,1,0:T(8,128)(2,1)S(1)}, u32[]{:S(2)}, u32[]{:S(2)}) collective-permute-start(bf16[16,8,128]{2,1,0:T(8,128)(2,1)S(1)} %get-tuple-element.12.after_ref), channel_id=1, source_target_pairs={{0,6},{1,7},{2,4},{3,5},{4,2},{5,3},{6,0},{7,1},{8,14},{9,15},{10,... | collective-permute-start | bytes 98312 | tf_op jit(solution)/shard_map/ppermute | solution.py:263
  19.6 4.8 %collective-permute-start.5 = (bf16[16,8,128]{2,1,0:T(8,128)(2,1)S(1)}, bf16[16,8,128]{2,1,0:T(8,128)(2,1)S(1)}, u32[]{:S(2)}, u32[]{:S(2)}) collective-permute-start(bf16[16,8,128]{2,1,0:T(8,128)(2,1)S(1)} %get-tuple-element.12.after_ref), channel_id=1, source_target_pairs={{0,4},{1,5},{2,6},{3,7},{4,0},{5,1},{6,2},{7,3},{8,12},{9,13},{10,... | collective-permute-start | bytes 98312 | tf_op jit(solution)/shard_map/ppermute | solution.py:263
  19.6 4.8 %collective-permute-start.4 = (bf16[16,8,128]{2,1,0:T(8,128)(2,1)S(1)}, bf16[16,8,128]{2,1,0:T(8,128)(2,1)S(1)}, u32[]{:S(2)}, u32[]{:S(2)}) collective-permute-start(bf16[16,8,128]{2,1,0:T(8,128)(2,1)S(1)} %get-tuple-element.12.after_ref), channel_id=1, source_target_pairs={{0,2},{1,3},{2,0},{3,1},{4,6},{5,7},{6,4},{7,5},{8,10},{9,11},{10,... | collective-permute-start | bytes 98312 | tf_op jit(solution)/shard_map/ppermute | solution.py:263
  24.4 5.7 %collective-permute-start.7 = (bf16[16,8,128]{2,1,0:T(8,128)(2,1)S(1)}, bf16[16,8,128]{2,1,0:T(8,128)(2,1)S(1)}, u32[]{:S(2)}, u32[]{:S(2)}) collective-permute-start(bf16[16,8,128]{2,1,0:T(8,128)(2,1)S(1)} %add_convert_fusion.1.xa_ref), channel_id=1, source_target_pairs={{0,1},{1,0},{2,3},{3,2},{4,5},{5,4},{6,7},{7,6},{8,9},{9,8},{10,11... | collective-permute-start | bytes 98312 | tf_op jit(solution)/shard_map/ppermute | solution.py:263
  48.8 5.6 %collective-permute-start.10 = (f32[4,4096]{1,0:T(4,128)S(1)}, f32[4,4096]{1,0:T(4,128)S(1)}, u32[]{:S(2)}, u32[]{:S(2)}) collective-permute-start(f32[4,4096]{1,0:T(4,128)S(1)} %get-tuple-element.10), channel_id=1, source_target_pairs={{0,24},{8,16},{16,8},{24,0},{1,25},{9,17},{17,9},{25,1},{2,26},{10... | collective-permute-start | bytes 196616 | tf_op jit(solution)/shard_map/ppermute | solution.py:263
  50.3 5.4 %collective-permute-start.9 = (f32[4,4096]{1,0:T(4,128)S(1)}, f32[4,4096]{1,0:T(4,128)S(1)}, u32[]{:S(2)}, u32[]{:S(2)}) collective-permute-start(f32[4,4096]{1,0:T(4,128)S(1)} %get-tuple-element.10), channel_id=1, source_target_pairs={{0,16},{8,24},{16,0},{24,8},{1,17},{9,25},{17,1},{25,9},{2,18},{10... | collective-permute-start | bytes 196616 | tf_op jit(solution)/shard_map/ppermute | solution.py:263
  51.5 4.3 %collective-permute-start.8 = (f32[4,4096]{1,0:T(4,128)S(1)}, f32[4,4096]{1,0:T(4,128)S(1)}, u32[]{:S(2)}, u32[]{:S(2)}) collective-permute-start(f32[4,4096]{1,0:T(4,128)S(1)} %get-tuple-element.10), channel_id=1, source_target_pairs={{0,8},{8,0},{16,24},{24,16},{1,9},{9,1},{17,25},{25,17},{2,10},{10... | collective-permute-start | bytes 196616 | tf_op jit(solution)/shard_map/ppermute | solution.py:263
  55.8 10.6 %copy-start = (bf16[4,4096]{1,0:T(4,128)(2,1)}, bf16[4,4096]{1,0:T(4,128)(2,1)S(1)}, u32[]{:S(2)}) copy-start(bf16[4,4096]{1,0:T(4,128)(2,1)S(1)} %add_convert_fusion.refs_0_) | copy-start | bytes 98308
  55.8 6.0 %collective-permute-start.16 = (bf16[4,4096]{1,0:T(4,128)(2,1)S(1)}, bf16[4,4096]{1,0:T(4,128)(2,1)S(1)}, u32[]{:S(2)}, u32[]{:S(2)}) collective-permute-start(bf16[4,4096]{1,0:T(4,128)(2,1)S(1)} %add_convert_fusion.refs_0_), channel_id=1, source_target_pairs={{0,6},{1,7},{2,4},{3,5},{4,2},{5,3},{6,0},{7,1},{8,14},{9,15},{10,... | collective-permute-start | bytes 98312 | tf_op jit(solution)/shard_map/ppermute | solution.py:263
  57.4 4.8 %collective-permute-start.14 = (bf16[4,4096]{1,0:T(4,128)(2,1)S(1)}, bf16[4,4096]{1,0:T(4,128)(2,1)S(1)}, u32[]{:S(2)}, u32[]{:S(2)}) collective-permute-start(bf16[4,4096]{1,0:T(4,128)(2,1)S(1)} %add_convert_fusion.refs_0_), channel_id=1, source_target_pairs={{0,4},{1,5},{2,6},{3,7},{4,0},{5,1},{6,2},{7,3},{8,12},{9,13},{10,... | collective-permute-start | bytes 98312 | tf_op jit(solution)/shard_map/ppermute | solution.py:263
  58.0 4.5 %collective-permute-start.12 = (bf16[4,4096]{1,0:T(4,128)(2,1)S(1)}, bf16[4,4096]{1,0:T(4,128)(2,1)S(1)}, u32[]{:S(2)}, u32[]{:S(2)}) collective-permute-start(bf16[4,4096]{1,0:T(4,128)(2,1)S(1)} %add_convert_fusion.refs_0_), channel_id=1, source_target_pairs={{0,2},{1,3},{2,0},{3,1},{4,6},{5,7},{6,4},{7,5},{8,10},{9,11},{10,... | collective-permute-start | bytes 98312 | tf_op jit(solution)/shard_map/ppermute | solution.py:263
  60.3 2.4 %collective-permute-start.11 = (bf16[4,4096]{1,0:T(4,128)(2,1)S(1)}, bf16[4,4096]{1,0:T(4,128)(2,1)S(1)}, u32[]{:S(2)}, u32[]{:S(2)}) collective-permute-start(bf16[4,4096]{1,0:T(4,128)(2,1)S(1)} %add_convert_fusion.refs_0_), channel_id=1, source_target_pairs={{0,1},{1,0},{2,3},{3,2},{4,5},{5,4},{6,7},{7,6},{8,9},{9,8},{10,11... | collective-permute-start | bytes 98312 | tf_op jit(solution)/shard_map/ppermute | solution.py:263
  61.8 1.2 %collective-permute-start.17 = (bf16[4,4096]{1,0:T(4,128)(2,1)S(1)}, bf16[4,4096]{1,0:T(4,128)(2,1)S(1)}, u32[]{:S(2)}, u32[]{:S(2)}) collective-permute-start(bf16[4,4096]{1,0:T(4,128)(2,1)S(1)} %collective-permute-done.16.refs_6_), channel_id=1, source_target_pairs={{0,1},{1,0},{2,3},{3,2},{4,5},{5,4},{6,7},{7,6},{8,9},{9,8},{10,11... | collective-permute-start | bytes 98312 | tf_op jit(solution)/shard_map/ppermute | solution.py:263
  62.2 1.2 %collective-permute-start.15 = (bf16[4,4096]{1,0:T(4,128)(2,1)S(1)}, bf16[4,4096]{1,0:T(4,128)(2,1)S(1)}, u32[]{:S(2)}, u32[]{:S(2)}) collective-permute-start(bf16[4,4096]{1,0:T(4,128)(2,1)S(1)} %collective-permute-done.14.refs_4_), channel_id=1, source_target_pairs={{0,1},{1,0},{2,3},{3,2},{4,5},{5,4},{6,7},{7,6},{8,9},{9,8},{10,11... | collective-permute-start | bytes 98312 | tf_op jit(solution)/shard_map/ppermute | solution.py:263
  62.5 1.2 %collective-permute-start.13 = (bf16[4,4096]{1,0:T(4,128)(2,1)S(1)}, bf16[4,4096]{1,0:T(4,128)(2,1)S(1)}, u32[]{:S(2)}, u32[]{:S(2)}) collective-permute-start(bf16[4,4096]{1,0:T(4,128)(2,1)S(1)} %collective-permute-done.12.refs_2_), channel_id=1, source_target_pairs={{0,1},{1,0},{2,3},{3,2},{4,5},{5,4},{6,7},{7,6},{8,9},{9,8},{10,11... | collective-permute-start | bytes 98312 | tf_op jit(solution)/shard_map/ppermute | solution.py:263
